TPU v7x, 256 devices: a whole 4x4x8 slice. The times are simulated.
256 devices in a mesh: lon: 32 (over z, y_lo, core), lat: 8 (over x, y_hi).
Axes of the slice: x: 4, y: 4 (y_hi: 2, y_lo: 2; y = y_hi * 2 + y_lo), z: 8, core: 2. Of those that a mesh axis runs over, the one named last changes fastest.
Arguments:
- embeddings: bfloat16 [512, 2048, 128], P('lat', 'lon'), may hold values from -400 to 400
- query_owner: int32 [2, 64], replicated, may hold values from 0 to 255
- query_row: int32 [2, 64], replicated, may hold values from 0 to 59
- query_col: int32 [2, 64], replicated, may hold values from 0 to 59
Outputs:
- scores: float32 [512, 2048, 128], P('lat', 'lon')
Inputs may be any that keep to these rules, and one draw needn't show every extreme that they name: `query_row`: the exemplar lies inside its owner's tile. `query_col`: the exemplar lies inside its owner's tile.
All inputs are finite; a program needn't handle non-finite values.
Results may differ from a plain program's by a relative error of at most 0.0029.
Values may be sent and summed in bfloat16 or wider, within the bound.
A program may use at most 128 MiB of HBM per device.

v0:
```python
import jax
import jax.numpy as jnp
from jax import lax
from jax.sharding import PartitionSpec as P


def extended_2(x, sides, width):
    for axis, dim in sides:
        count, length = (lax.axis_size(axis), x.shape[dim])
        up = [(i, (i + 1) % count) for i in range(count)]
        down = [(j, i) for i, j in up]
        last = lax.slice_in_dim(x, length - width, length, axis=dim)
        first = lax.slice_in_dim(x, 0, width, axis=dim)
        before = lax.ppermute(last, axis, up)
        after = lax.ppermute(first, axis, down)
        x = jnp.concatenate([before, x, after], axis=dim)
    return x


def body(embeddings, query_owner, query_row, query_col):
    rows, cols, chans = embeddings.shape
    band = lax.axis_index("lat")
    strip = lax.axis_index("lon")
    here = band * lax.axis_size("lon") + strip
    owner = query_owner.reshape(-1)
    row_first = query_row.reshape(-1)
    col_first = query_col.reshape(-1)

    def take(row_one, col_one):
        zero = jnp.zeros((), jnp.int32)
        return lax.dynamic_slice(embeddings, (row_one, col_one, zero), (5, 5, chans))

    patches = jax.vmap(take, out_axes=3)(row_first, col_first).astype(jnp.float32)
    count = patches.shape[3]
    table = jnp.where((owner == here)[None, None, None, :], patches, 0.0)
    whole = lax.psum(table, ("lon", "lat"))
    mean_sq = jnp.mean(whole * whole, axis=(0, 1, 2))
    queries = (whole * lax.rsqrt(mean_sq + 1e-05)).astype(jnp.bfloat16)
    extended = extended_2(embeddings, (("lat", 0), ("lon", 1)), 2)
    row_index = jnp.arange(rows + 4, dtype=jnp.int32)[:, None, None]
    cut_top = (band == 0) & (row_index < 2)
    cut_bottom = (band == lax.axis_size("lat") - 1) & (row_index >= rows + 2)
    extended = jnp.where(cut_top | cut_bottom, jnp.zeros((), jnp.bfloat16), extended)
    total = jnp.zeros((rows * cols, count), jnp.float32)
    for shift_y in range(5):
        for shift_x in range(5):
            slab = extended[shift_y : shift_y + rows, shift_x : shift_x + cols, :].reshape(
                rows * cols, chans
            )
            total = total + jnp.dot(
                slab, queries[shift_y, shift_x], preferred_element_type=jnp.float32
            )
    squares = jnp.sum(jnp.square(extended.astype(jnp.float32)), axis=2)
    box_sum = jnp.zeros((rows, cols), jnp.float32)
    for shift_y in range(5):
        for shift_x in range(5):
            box_sum = box_sum + squares[shift_y : shift_y + rows, shift_x : shift_x + cols]
    energy = box_sum / (25 * chans)
    return total.reshape(rows, cols, count) * lax.rsqrt(25 * chans * (energy + 1e-05))[:, :, None]


def solution(mesh):
    placed = (P("lat", "lon", None), P(), P(), P())
    return jax.shard_map(
        body, mesh=mesh, in_specs=placed, out_specs=P("lat", "lon", None), check_vma=False
    )
```

profile of v0, /device:TPU:2, one launch (start us, length us, event | category | flops | bytes accessed | tf_op | source)
XLA Modules:
  0.0 670.3 jit_solution(10743078012196713790)
XLA Ops:
  7.3 3.2 collective-permute-start.1
  13.2 350.3 %while.1 = (s32[]{:T(128)}, bf16[64,64,128]{2,1,0:T(8,128)(2,1)}, s32[128,3]{0,1:T(4,128)S(1)}, bf16[128,5,5,128]{3,2,1,0:T(8,128)(2,1)S(1)}, s32[]{:T(128)}) while((s32[]{:T(128)}, bf16[64,64,128]{2,1,0:T(8,128)(2,1)}, s32[128,3]{0,1:T(4,128)S(1)}, bf16[128,5,5,128]{3,2,1,0:T(8,128)(2,1)S(1)}, s32[]{:T(128)}) %tuple.46), condition=%wide.while_cond, body=%wide.while_body.sunk | while | flops 2 | bytes 16765 | solution.py:31
  13.8 2.1 bitcast_dynamic-update-slice_fusion.2
  16.6 2.1 bitcast_dynamic-update-slice_fusion.2
  19.3 2.1 bitcast_dynamic-update-slice_fusion.2
  22.1 2.1 bitcast_dynamic-update-slice_fusion.2
  24.8 2.1 bitcast_dynamic-update-slice_fusion.2
  27.5 2.1 bitcast_dynamic-update-slice_fusion.2
  49.4 2.1 bitcast_dynamic-update-slice_fusion.2
  52.2 2.1 bitcast_dynamic-update-slice_fusion.2
  54.9 2.1 bitcast_dynamic-update-slice_fusion.2
  57.7 2.1 bitcast_dynamic-update-slice_fusion.2
  60.4 2.1 bitcast_dynamic-update-slice_fusion.2
  63.1 2.1 bitcast_dynamic-update-slice_fusion.2
  65.9 2.1 bitcast_dynamic-update-slice_fusion.2
  68.6 2.1 bitcast_dynamic-update-slice_fusion.2
  71.4 2.1 bitcast_dynamic-update-slice_fusion.2
  76.8 2.1 bitcast_dynamic-update-slice_fusion.2
  79.5 2.1 bitcast_dynamic-update-slice_fusion.2
  82.3 2.1 bitcast_dynamic-update-slice_fusion.2
  85.0 2.1 bitcast_dynamic-update-slice_fusion.2
  87.8 2.1 bitcast_dynamic-update-slice_fusion.2
  109.7 2.1 bitcast_dynamic-update-slice_fusion.2
  112.4 2.1 bitcast_dynamic-update-slice_fusion.2
  115.1 2.1 bitcast_dynamic-update-slice_fusion.2
  117.9 2.1 bitcast_dynamic-update-slice_fusion.2
  120.6 2.1 bitcast_dynamic-update-slice_fusion.2
  268.4 2.1 bitcast_dynamic-update-slice_fusion.2
  366.7 5.8 collective-permute-start.3
  375.8 3.4 fusion.7
  379.2 8.0 %fusion.6 = (bf16[64,64,128]{2,1,0:T(8,128)(2,1)S(1)}, bf16[64,64,128]{2,1,0:T(8,128)(2,1)S(1)}, bf16[64,64,128]{2,1,0:T(8,128)(2,1)S(1)}, bf16[64,64,128]{2,1,0...) fusion(bf16[68,68,128]{2,1,0:T(8,128)(2,1)S(1)} %get-tuple-elem, ...), kind=kLoop, calls=%fused_computation.96 | loop fusion | bytes 39845888 | tf_op jit(solution)/shard_map/slice | solution.py:47
  387.3 244.6 %all-reduce.2.cloned.1.call-done = f32[5,5,128,128]{3,2,1,0:T(8,128)} async-done(((f32[5,5,128,128]{3,2,1,0:T(8,128)}), f32[5,5,128,128]{3,2,1,0:T(8,128)}) %all-reduce.2.cloned.1.call-update) | async-done | bytes 1638416 | tf_op jit(solution)/shard_map/psum | solution.py:36
  (461 shorter events, 336.3 us)
Async XLA Ops:
  6.5 625.3 %all-reduce.2.cloned.1.call-start = ((), (), s32[]{:S(2)}) async-start(), calls=%async_computation | async-start | bytes 3276800 | tf_op jit(solution)/shard_map/psum | solution.py:36
  7.3 359.2 %collective-permute-start.1 = (bf16[2,64,128]{2,1,0:T(8,128)(2,1)S(1)}, bf16[2,64,128]{2,1,0:T(8,128)(2,1)S(1)}, u32[]{:S(2)}, u32[]{:S(2)}) collective-permute-start(bf16[2,64,128]{2,1,0:T(8,128)(2,1)S(1)} %get-tuple-element.52), channel_id=1, source_target_pairs={{1,0},{2,1},{3,2},{4,3},{5,4},{6,5},{7,6},{0,7},{9,8},{10,9},{11,1... | collective-permute-start | bytes 98312 | tf_op jit(solution)/shard_map/ppermute | solution.py:15
  10.5 355.8 %collective-permute-start = (bf16[2,64,128]{2,1,0:T(8,128)(2,1)S(1)}, bf16[2,64,128]{2,1,0:T(8,128)(2,1)S(1)}, u32[]{:S(2)}, u32[]{:S(2)}) collective-permute-start(bf16[2,64,128]{2,1,0:T(8,128)(2,1)S(1)} %get-tuple-element.53), channel_id=1, source_target_pairs={{0,1},{1,2},{2,3},{3,4},{4,5},{5,6},{6,7},{7,0},{8,9},{9,10},{10,1... | collective-permute-start | bytes 98312 | tf_op jit(solution)/shard_map/ppermute | solution.py:14
  364.9 1.5 copy-start.23
  366.6 7.4 %collective-permute-start.2 = (bf16[68,2,128]{2,1,0:T(2,128)(2,1)S(1)}, bf16[68,2,128]{2,1,0:T(2,128)(2,1)S(1)}, u32[]{:S(2)}, u32[]{:S(2)}) collective-permute-start(bf16[68,2,128]{2,1,0:T(2,128)(2,1)S(1)} %get-tuple-element.50), channel_id=1, source_target_pairs={{0,8},{8,16},{16,24},{24,32},{32,40},{40,48},{48,56},{56,64},{64,7... | collective-permute-start | bytes 104456 | tf_op jit(solution)/shard_map/ppermute | solution.py:14
  366.7 7.4 %collective-permute-start.3 = (bf16[68,2,128]{2,1,0:T(2,128)(2,1)S(1)}, bf16[68,2,128]{2,1,0:T(2,128)(2,1)S(1)}, u32[]{:S(2)}, u32[]{:S(2)}) collective-permute-start(bf16[68,2,128]{2,1,0:T(2,128)(2,1)S(1)} %get-tuple-element.51), channel_id=1, source_target_pairs={{8,0},{16,8},{24,16},{32,24},{40,32},{48,40},{56,48},{64,56},{72,6... | collective-permute-start | bytes 104456 | tf_op jit(solution)/shard_map/ppermute | solution.py:15
  631.8 2.0 copy-start
  631.8 2.3 copy-start.22
  634.1 1.2 copy-start.21
  635.3 1.2 copy-start.20
  636.6 1.2 copy-start.19
  637.8 1.2 copy-start.18
  639.0 1.2 copy-start.17
  640.2 1.2 copy-start.16
  641.5 1.2 copy-start.15
  642.7 1.2 copy-start.14
  643.9 1.2 copy-start.13
  645.1 1.2 copy-start.12
  646.4 1.2 copy-start.11
  647.6 1.2 copy-start.10
  648.8 1.2 copy-start.9
  650.0 1.2 copy-start.8
  651.3 1.2 copy-start.7
  652.5 1.2 copy-start.6
  653.7 1.2 copy-start.5
  654.9 1.2 copy-start.4
  656.2 1.2 copy-start.3
  657.4 1.2 copy-start.2
  658.6 1.2 copy-start.1
Sparse Core Ops, SparseCore 0:
  366.4 265.3 all-reduce.1
where the time goes:
time: 681 us; the launch traced here: 670 us
  local copies, waits for them, and re-layouts  381 us (56%)
  waiting for transfers between devices  246 us (36%)
  between operations  13.7 us (2%)
  matrix products  10.3 us (2%)
  starting transfers between devices  9.44 us (1%)
  other arithmetic  7.83 us (1%)
    gather x384, local copies, waits for them, and re-layouts  348 us
    psum x1, waiting for transfers between devices, body(): whole = lax.psum(table, ('lon', 'lat'))  245 us
    unnamed x50, local copies, waits for them, and re-layouts  17.1 us
  transfers between devices with their start and end apart: 5, of which 3 were waited for; matrix products, arithmetic and copies ran while one was open for 55% of the time, Pallas kernels for 0%

commit v1 on v0

--- a/solution.py
+++ b/solution.py
@@ -33,7 +33,7 @@
     patches = jax.vmap(take, out_axes=3)(row_first, col_first).astype(jnp.float32)
     count = patches.shape[3]
     table = jnp.where((owner == here)[None, None, None, :], patches, 0.0)
-    whole = lax.psum(table, ("lon", "lat"))
+    whole = lax.psum(lax.psum(table, "lon"), "lat")
     mean_sq = jnp.mean(whole * whole, axis=(0, 1, 2))
     queries = (whole * lax.rsqrt(mean_sq + 1e-05)).astype(jnp.bfloat16)
     extended = extended_2(embeddings, (("lat", 0), ("lon", 1)), 2)

time: 681 us -> 744 us (1.093)
  waiting for transfers between devices: 246 us -> 314 us
    psum x1 -> x2, waiting for transfers between devices: 245 us -> 309 us  [body(): whole = lax.psum(lax.psum(table, 'lon'), 'lat')]
    unnamed x50 -> x52, local copies, waits for them, and re-layouts: 17.1 us -> 17.9 us
  transfers between devices with their start and end apart: 5 -> 6, of which waited for: 3 -> 6; matrix products, arithmetic and copies ran while one was open for 55% -> 2% of each run, Pallas kernels for 0% -> 0%
where the time goes in v1:
time: 744 us; the launch traced here: 733 us
  local copies, waits for them, and re-layouts  376 us (51%)
  waiting for transfers between devices  314 us (42%)
  between operations  13.7 us (2%)
  matrix products  10.3 us (1%)
  starting transfers between devices  9.01 us (1%)
  other arithmetic  7.82 us (1%)
    gather x384, local copies, waits for them, and re-layouts  344 us
    psum x2, waiting for transfers between devices, body(): whole = lax.psum(lax.psum(table, 'lon'), 'lat')  309 us
    unnamed x52, local copies, waits for them, and re-layouts  17.9 us
  transfers between devices with their start and end apart: 6, of which 6 were waited for; matrix products, arithmetic and copies ran while one was open for 2% of the time, Pallas kernels for 0%

profile of v1, /device:TPU:2, one launch (start us, length us, event | category | flops | bytes accessed | tf_op | source)
XLA Modules:
  0.0 733.0 jit_solution(15044461541552999141)
XLA Ops:
  8.8 345.5 %while.1 = (s32[]{:T(128)}, bf16[64,64,128]{2,1,0:T(8,128)(2,1)}, s32[128,3]{0,1:T(4,128)S(1)}, bf16[128,5,5,128]{3,2,1,0:T(8,128)(2,1)S(1)}, s32[]{:T(128)}) while((s32[]{:T(128)}, bf16[64,64,128]{2,1,0:T(8,128)(2,1)}, s32[128,3]{0,1:T(4,128)S(1)}, bf16[128,5,5,128]{3,2,1,0:T(8,128)(2,1)S(1)}, s32[]{:T(128)}) %tuple.46), condition=%wide.while_cond, body=%wide.while_body.sunk | while | flops 2 | bytes 16765 | solution.py:31
  9.5 2.0 bitcast_dynamic-update-slice_fusion.2
  14.9 2.0 bitcast_dynamic-update-slice_fusion.2
  17.7 2.0 bitcast_dynamic-update-slice_fusion.2
  25.8 2.0 bitcast_dynamic-update-slice_fusion.2
  33.9 2.0 bitcast_dynamic-update-slice_fusion.2
  42.0 2.0 bitcast_dynamic-update-slice_fusion.2
  47.4 2.0 bitcast_dynamic-update-slice_fusion.2
  55.5 2.0 bitcast_dynamic-update-slice_fusion.2
  63.6 2.0 bitcast_dynamic-update-slice_fusion.2
  77.1 2.0 bitcast_dynamic-update-slice_fusion.2
  82.5 2.0 bitcast_dynamic-update-slice_fusion.2
  90.6 2.0 bitcast_dynamic-update-slice_fusion.2
  98.7 2.0 bitcast_dynamic-update-slice_fusion.2
  106.8 2.0 bitcast_dynamic-update-slice_fusion.2
  112.2 2.0 bitcast_dynamic-update-slice_fusion.2
  120.3 2.0 bitcast_dynamic-update-slice_fusion.2
  128.4 2.0 bitcast_dynamic-update-slice_fusion.2
  133.8 2.0 bitcast_dynamic-update-slice_fusion.2
  141.9 2.0 bitcast_dynamic-update-slice_fusion.2
  147.3 2.0 bitcast_dynamic-update-slice_fusion.2
  150.0 2.0 bitcast_dynamic-update-slice_fusion.2
  266.0 2.0 bitcast_dynamic-update-slice_fusion.2
  349.7 2.0 bitcast_dynamic-update-slice_fusion.2
  357.4 3.2 collective-permute-start
  363.9 2.2 collective-permute-done.1
  366.2 4.4 collective-permute-start.3
  373.6 211.7 %all-reduce.3.cloned.1.call-done = f32[5,5,128,128]{3,2,1,0:T(8,128)} async-done(((f32[5,5,128,128]{3,2,1,0:T(8,128)}), f32[5,5,128,128]{3,2,1,0:T(8,128)}) %all-reduce.3.cloned.1.call-update) | async-done | bytes 1638416 | tf_op jit(solution)/shard_map/psum | solution.py:36
  585.6 3.5 fusion.7
  589.0 7.7 %fusion.6 = (bf16[64,64,128]{2,1,0:T(8,128)(2,1)S(1)}, bf16[64,64,128]{2,1,0:T(8,128)(2,1)S(1)}, bf16[64,64,128]{2,1,0:T(8,128)(2,1)}, bf16[64,64,128]{2,1,0:T(8...) fusion(bf16[68,68,128]{2,1,0:T(8,128)(2,1)S(1)} %get-tuple-elem, ...), kind=kLoop, calls=%fused_computation.96 | loop fusion | bytes 39845888 | tf_op jit(solution)/shard_map/slice | solution.py:47
  596.7 97.0 %all-reduce.5.cloned.1.call-done = f32[5,5,128,128]{3,2,1,0:T(8,128)} async-done(((f32[5,5,128,128]{3,2,1,0:T(8,128)}), f32[5,5,128,128]{3,2,1,0:T(8,128)}) %all-reduce.5.cloned.1.call-update) | async-done | bytes 1638416 | tf_op jit(solution)/shard_map/psum | solution.py:36
  693.7 2.0 multiply_reduce_fusion.1
  (466 shorter events, 339.4 us)
Async XLA Ops:
  6.5 578.8 %all-reduce.3.cloned.1.call-start = ((), (), s32[]{:S(2)}) async-start(), calls=%async_computation | async-start | bytes 3276800 | tf_op jit(solution)/shard_map/psum | solution.py:36
  355.9 1.5 copy-start.24
  357.2 336.5 %all-reduce.5.cloned.1.call-start = ((), (), s32[]{:S(2)}) async-start(), calls=%async_computation.1 | async-start | bytes 3276800 | tf_op jit(solution)/shard_map/psum | solution.py:36
  357.4 6.4 collective-permute-start
  360.6 5.4 collective-permute-start.1
  366.1 6.0 collective-permute-start.2
  366.2 6.1 collective-permute-start.3
  693.7 2.0 copy-start
  693.7 2.3 copy-start.23
  696.0 1.2 copy-start.22
  697.2 1.2 copy-start.21
  698.4 1.2 copy-start.20
  699.7 1.2 copy-start.19
  700.9 1.2 copy-start.18
  702.1 1.2 copy-start.17
  703.3 1.2 copy-start.16
  704.6 1.2 copy-start.15
  705.8 1.2 copy-start.14
  707.0 1.2 copy-start.13
  708.2 1.2 copy-start.12
  709.5 1.2 copy-start.11
  710.7 1.2 copy-start.10
  711.9 1.2 copy-start.9
  713.1 1.2 copy-start.8
  714.4 1.2 copy-start.7
  715.6 1.2 copy-start.6
  716.8 1.2 copy-start.5
  718.0 1.2 copy-start.4
  719.3 1.2 copy-start.3
  720.5 1.2 copy-start.2
  721.7 1.2 copy-start.1
Sparse Core Ops, SparseCore 0:
  357.4 227.8 all-reduce.2
  588.2 105.5 all-reduce.4
